TPU v7x, 32 devices: a whole 2x2x4 slice. The times are simulated.
32 devices in a mesh: replica: 16 (over z, y, x), dom: 2 (over core).
Axes of the slice: x: 2, y: 2, z: 4, core: 2. Of those that a mesh axis runs over, the one named last changes fastest.
Arguments:
- inputs: bfloat16 [2, 384, 8192], P(None, 'replica', 'dom'), may hold values from -6 to 6
- targets: bfloat16 [2, 384, 8192], P(None, 'replica', 'dom'), may hold values from -0.8984375 to 0.8984375
- w_first: float32 [8192, 8192], P('replica', 'dom'), may hold values from -5 to 5
- acc_first: float32 [8192, 8192], P('replica', 'dom'), may hold values from 0.5 to 8
- w_second: float32 [8192, 8192], P('dom', 'replica'), may hold values from -5 to 5
- acc_second: float32 [8192, 8192], P('dom', 'replica'), may hold values from 0.5 to 8
Outputs:
- new_first: float32 [8192, 8192], P('replica', 'dom')
- new_acc_first: float32 [8192, 8192], P('replica', 'dom')
- new_second: float32 [8192, 8192], P('dom', 'replica')
- new_acc_second: float32 [8192, 8192], P('dom', 'replica')
All inputs are finite; a program needn't handle non-finite values.
Results may differ from a plain program's by a relative error of at most 0.015.
Values may be sent and summed in bfloat16 or wider, within the bound.
No kernel may reach another device: no remote copies, remote signals or barrier semaphores. Data moves between devices by JAX's collectives and lax.ppermute only.
A program may use at most 192 MiB of HBM per device.

v0:
```python
import math
import jax
import jax.numpy as jnp
from jax import lax
from jax.sharding import PartitionSpec as P

learn_rate = 0.05
error_weight = 0.25


def local(inputs, targets, w_first, acc_first, w_second, acc_second):
    full_width = w_first.shape[1] * lax.axis_size("dom")
    unit_scale = 1.0 / math.sqrt(0.4 * full_width)
    for round_index in range(inputs.shape[0]):
        first_half = w_first.astype(jnp.bfloat16)
        second_half = w_second.astype(jnp.bfloat16)
        round_batch = lax.all_gather(inputs[round_index], "replica", axis=0, tiled=True)
        goal_rows = targets[round_index]
        first_terms = (
            lax.dot_general(
                round_batch,
                first_half,
                (((1,), (1,)), ((), ())),
                preferred_element_type=jnp.float32,
            )
            * unit_scale
        )
        first_out = jnp.tanh(lax.psum(first_terms.astype(jnp.bfloat16), "dom").astype(jnp.float32))
        first_rows = first_out.astype(jnp.bfloat16)
        second_out = jnp.tanh(
            lax.psum_scatter(
                lax.dot_general(
                    first_rows,
                    second_half,
                    (((1,), (1,)), ((), ())),
                    preferred_element_type=jnp.float32,
                )
                * unit_scale,
                "replica",
                scatter_dimension=0,
                tiled=True,
            )
        )
        error_own = (
            (second_out - goal_rows.astype(jnp.float32))
            * error_weight
            * (1.0 - second_out * second_out)
        ).astype(jnp.bfloat16)
        error_half = lax.all_gather(error_own, "replica", axis=0, tiled=True)
        second_grad = lax.dot_general(
            error_half, first_rows, (((0,), (0,)), ((), ())), preferred_element_type=jnp.float32
        )
        back_terms = (
            jnp.dot(error_half, second_half, preferred_element_type=jnp.float32) * unit_scale
        )
        back_pre = lax.psum(back_terms.astype(jnp.bfloat16), "dom").astype(jnp.float32)
        first_error = (back_pre * (1.0 - first_out * first_out)).astype(jnp.bfloat16)
        first_grad = lax.dot_general(
            first_error, round_batch, (((0,), (0,)), ((), ())), preferred_element_type=jnp.float32
        )
        acc_first = acc_first + first_grad * first_grad
        w_first = w_first - learn_rate * first_grad / jnp.sqrt(acc_first)
        acc_second = acc_second + second_grad * second_grad
        w_second = w_second - learn_rate * second_grad / jnp.sqrt(acc_second)
    return (w_first, acc_first, w_second, acc_second)


def solution(mesh):
    placed = (
        P(None, "replica", "dom"),
        P(None, "replica", "dom"),
        P("replica", "dom"),
        P("replica", "dom"),
        P("dom", "replica"),
        P("dom", "replica"),
    )
    return jax.shard_map(
        local,
        mesh=mesh,
        in_specs=placed,
        out_specs=(
            P("replica", "dom"),
            P("replica", "dom"),
            P("dom", "replica"),
            P("dom", "replica"),
        ),
        check_vma=False,
    )
```

profile of v0, /device:TPU:0, one launch (start us, length us, event | category | flops | bytes accessed | tf_op | source)
XLA Modules:
  0.0 729.3 jit_solution(1402167555871297250)
XLA Ops:
  7.2 1.8 fusion.71
  9.1 73.1 %all-gather.11.cloned.1.call-done = bf16[1,384,4096]{2,1,0:T(8,128)(2,1)} async-done(((bf16[1,24,4096]{2,1,0:T(8,128)(2,1)}), bf16[1,384,4096]{2,1,0:T(8,128)(2,1)}) %all-gather.11.cloned.1.call-update) | async-done | bytes 3145744 | tf_op jit(solution)/shard_map/all_gather | solution.py:17
  82.2 6.9 fusion.37
  89.2 17.1 %all-reduce.5.cloned.1.call-done = bf16[384,512]{1,0:T(8,128)(2,1)} async-done(((bf16[384,512]{1,0:T(8,128)(2,1)}), bf16[384,512]{1,0:T(8,128)(2,1)}) %all-reduce.5.cloned.1.call-update) | async-done | bytes 393232 | tf_op jit(solution)/shard_map/psum | solution.py:28
  106.3 8.1 %convolution_multiply_fusion.1 = f32[384,4096]{1,0:T(8,128)} fusion(f32[4096,512]{1,0:T(8,128)} %param.10, bf16[384,512]{1,0:T(8,128)(2,1)} %all-reduce.5.cloned.1.call-done), kind=kOutput, calls=%fused_computation.9 | convolution fusion | flops 1614675968 | bytes 15073280 | tf_op jit(solution)/shard_map/dot_general | solution.py:32
  114.4 147.1 %reduce-scatter.3.cloned.1.call-done = f32[24,4096]{1,0:T(8,128)} async-done(((f32[384,4096]{1,0:T(8,128)}), f32[24,4096]{1,0:T(8,128)}) %reduce-scatter.3.cloned.1.call-update) | async-done | bytes 393232 | tf_op jit(solution)/shard_map/reduce_scatter | solution.py:31
  261.5 1.8 fusion.60
  263.4 69.0 %all-gather.7.cloned.1.call-done = bf16[384,4096]{1,0:T(8,128)(2,1)} async-done(((bf16[24,4096]{1,0:T(8,128)(2,1)}), bf16[384,4096]{1,0:T(8,128)(2,1)}) %all-gather.7.cloned.1.call-update) | async-done | bytes 3145744 | tf_op jit(solution)/shard_map/all_gather | solution.py:49
  332.4 6.9 fusion.45
  339.3 0.5 all-gather.13.cloned.1.call-update
  339.9 16.5 %all-reduce.7.cloned.1.call-done = bf16[384,512]{1,0:T(8,128)(2,1)} async-done(((bf16[384,512]{1,0:T(8,128)(2,1)}), bf16[384,512]{1,0:T(8,128)(2,1)}) %all-reduce.7.cloned.1.call-update) | async-done | bytes 393232 | tf_op jit(solution)/shard_map/psum | solution.py:56
  356.4 6.8 fusion.7
  363.2 65.8 %all-gather.13.cloned.1.call-done = bf16[1,384,4096]{2,1,0:T(8,128)(2,1)} async-done(((bf16[1,24,4096]{2,1,0:T(8,128)(2,1)}), bf16[1,384,4096]{2,1,0:T(8,128)(2,1)}) %all-gather.13.cloned.1.call-update) | async-done | bytes 3145744 | tf_op jit(solution)/shard_map/all_gather | solution.py:17
  429.0 12.2 %fusion.48 = bf16[384,512]{1,0:T(8,128)(2,1)} fusion(bf16[1,384,4096]{2,1,0:T(8,128)(2,1)} %all-gather.13.cloned.1.call-done, f32[512,4096]{1,0:T(8,128)} %param.8, f32[512,4096]{1,0:T(8,128)} %fusion.7, f32[512,4096]{1,0:T(8,128)} %param.9), kind=kOutput, calls=%fused_computation.34 | convolution fusion | flops 1623588864 | bytes 28704768 | tf_op jit(solution)/shard_map/dot_general | solution.py:20
  441.4 11.2 %multiply_subtract_fusion.2 = (f32[4096,512]{1,0:T(8,128)}, f32[4096,512]{1,0:T(8,128)}) fusion(f32[4096,512]{1,0:T(8,128)} %param.10, f32[4096,512]{1,0:T(8,128)} %param.11, bf16[384,4096]{1,0:T(8,128)(2,1)S(1)} %copy-done.1, bf16[384,512]{1,0:T(8,128)(2,1)S(1)} %copy-done.4), kind=kOutput, calls=%fused_computation.4 | convolution fusion | flops 1621491712 | bytes 37093376 | tf_op jit(solution)/shard_map/dot_general | solution.py:50
  452.6 5.7 all-reduce.9.cloned.1.call-done
  458.3 8.1 %convolution_multiply_fusion = f32[384,4096]{1,0:T(8,128)} fusion(f32[4096,512]{1,0:T(8,128)} %get-tuple-element.10, bf16[384,512]{1,0:T(8,128)(2,1)} %all-reduce.9.cloned.1.call-done), kind=kOutput, calls=%fused_computation.8 | convolution fusion | flops 1614675968 | bytes 15073280 | tf_op jit(solution)/shard_map/dot_general | solution.py:32
  466.5 146.6 %reduce-scatter.5.cloned.1.call-done = f32[24,4096]{1,0:T(8,128)} async-done(((f32[384,4096]{1,0:T(8,128)}), f32[24,4096]{1,0:T(8,128)}) %reduce-scatter.5.cloned.1.call-update) | async-done | bytes 393232 | tf_op jit(solution)/shard_map/reduce_scatter | solution.py:31
  613.1 1.8 fusion.57
  615.0 69.2 %all-gather.9.cloned.1.call-done = bf16[384,4096]{1,0:T(8,128)(2,1)} async-done(((bf16[24,4096]{1,0:T(8,128)(2,1)}), bf16[384,4096]{1,0:T(8,128)(2,1)}) %all-gather.9.cloned.1.call-update) | async-done | bytes 3145744 | tf_op jit(solution)/shard_map/all_gather | solution.py:49
  684.2 6.9 fusion.42
  691.1 14.7 %multiply_subtract_fusion = (f32[4096,512]{1,0:T(8,128)}, f32[4096,512]{1,0:T(8,128)}) fusion(f32[4096,512]{1,0:T(8,128)} %get-tuple-element.10, f32[4096,512]{1,0:T(8,128)} %param.11, f32[4096,512]{1,0:T(8,128)} %get-tuple-element.11, bf16[384,4096]{1,0:T(8,128)(2,1)} %all-gather.9.cloned.1.call-done, bf16[384,512]{1,0:T(8,128)(2,1)S(1)} %copy-done.3), kind=kOutput, calls=%fused_computation | convolution fusion | flops 1625686016 | bytes 45481984 | tf_op jit(solution)/shard_map/dot_general | solution.py:50
  705.8 2.4 all-reduce.11.cloned.1.call-done
  708.2 14.2 %multiply_subtract_fusion.1 = (f32[512,4096]{1,0:T(8,128)}, f32[512,4096]{1,0:T(8,128)}) fusion(f32[512,4096]{1,0:T(8,128)} %param.8, f32[512,4096]{1,0:T(8,128)} %param.9, f32[512,4096]{1,0:T(8,128)} %fusion.7, bf16[1,384,4096]{2,1,0:T(8,128)(2,1)S(1)} %copy-done, bf16[384,512]{1,0:T(8,128)(2,1)} %all-reduce.11.cloned.1.call-done, ...), kind=kOutput, calls=%fused_computation.2 | convolution fusion | flops 1632763904 | bytes 45875200 | tf_op jit(solution)/shard_map/dot_general | solution.py:58
  (31 shorter events, 0.8 us)
Async XLA Ops:
  7.2 75.1 %all-gather.11.cloned.1.call-start = ((), (), s32[]{:S(2)}) async-start(), calls=%async_computation.10 | async-start | bytes 3342336 | tf_op jit(solution)/shard_map/all_gather | solution.py:17
  9.0 97.3 %all-reduce.5.cloned.1.call-start = ((), (), s32[]{:S(2)}) async-start(), calls=%async_computation.2 | async-start | bytes 786432 | tf_op jit(solution)/shard_map/psum | solution.py:28
  89.2 172.4 %reduce-scatter.3.cloned.1.call-start = ((), (), s32[]{:S(2)}) async-start(), calls=%async_computation.3 | async-start | bytes 6684672 | tf_op jit(solution)/shard_map/reduce_scatter | solution.py:31
  114.4 242.1 %copy-start.2 = (bf16[1,384,4096]{2,1,0:T(8,128)(2,1)S(1)}, bf16[1,384,4096]{2,1,0:T(8,128)(2,1)}, u32[]{:S(2)}) copy-start(bf16[1,384,4096]{2,1,0:T(8,128)(2,1)} %all-gather.11.cloned.1.call-done) | copy-start | bytes 9437188
  114.4 242.1 %copy-start.4 = (bf16[384,512]{1,0:T(8,128)(2,1)S(1)}, bf16[384,512]{1,0:T(8,128)(2,1)}, u32[]{:S(2)}) copy-start(bf16[384,512]{1,0:T(8,128)(2,1)} %all-reduce.5.cloned.1.call-done) | copy-start | bytes 1179652
  114.4 218.0 %all-gather.7.cloned.1.call-start = ((), (), s32[]{:S(2)}) async-start(), calls=%async_computation.4 | async-start | bytes 3342336 | tf_op jit(solution)/shard_map/all_gather | solution.py:49
  263.4 93.0 %all-reduce.7.cloned.1.call-start = ((), (), s32[]{:S(2)}) async-start(), calls=%async_computation.5 | async-start | bytes 786432 | tf_op jit(solution)/shard_map/psum | solution.py:56
  339.3 89.7 %all-gather.13.cloned.1.call-start = ((), (), s32[]{:S(2)}) async-start(), calls=%async_computation.11 | async-start | bytes 3342336 | tf_op jit(solution)/shard_map/all_gather | solution.py:17
  339.9 118.5 %all-reduce.9.cloned.1.call-start = ((), (), s32[]{:S(2)}) async-start(), calls=%async_computation.6 | async-start | bytes 786432 | tf_op jit(solution)/shard_map/psum | solution.py:28
  363.2 78.2 %copy-start.1 = (bf16[384,4096]{1,0:T(8,128)(2,1)S(1)}, bf16[384,4096]{1,0:T(8,128)(2,1)}, u32[]{:S(2)}) copy-start(bf16[384,4096]{1,0:T(8,128)(2,1)} %all-gather.7.cloned.1.call-done) | copy-start | bytes 9437188
  441.2 171.9 %reduce-scatter.5.cloned.1.call-start = ((), (), s32[]{:S(2)}) async-start(), calls=%async_computation.7 | async-start | bytes 6684672 | tf_op jit(solution)/shard_map/reduce_scatter | solution.py:31
  458.3 154.8 %copy-start.5 = (bf16[2,24,4096]{2,1,0:T(8,128)(2,1)S(1)}, bf16[2,24,4096]{2,1,0:T(8,128)(2,1)}, u32[]{:S(2)}) copy-start(bf16[2,24,4096]{2,1,0:T(8,128)(2,1)} %param.7) | copy-start | bytes 1179652
  466.4 224.6 %copy-start.3 = (bf16[384,512]{1,0:T(8,128)(2,1)S(1)}, bf16[384,512]{1,0:T(8,128)(2,1)}, u32[]{:S(2)}) copy-start(bf16[384,512]{1,0:T(8,128)(2,1)} %all-reduce.9.cloned.1.call-done) | copy-start | bytes 1179652
  466.5 217.7 %all-gather.9.cloned.1.call-start = ((), (), s32[]{:S(2)}) async-start(), calls=%async_computation.8 | async-start | bytes 3342336 | tf_op jit(solution)/shard_map/all_gather | solution.py:49
  614.9 93.3 %all-reduce.11.cloned.1.call-start = ((), (), s32[]{:S(2)}) async-start(), calls=%async_computation.9 | async-start | bytes 786432 | tf_op jit(solution)/shard_map/psum | solution.py:56
  691.1 17.1 %copy-start = (bf16[1,384,4096]{2,1,0:T(8,128)(2,1)S(1)}, bf16[1,384,4096]{2,1,0:T(8,128)(2,1)}, u32[]{:S(2)}) copy-start(bf16[1,384,4096]{2,1,0:T(8,128)(2,1)} %all-gather.13.cloned.1.call-done) | copy-start | bytes 9437188
Sparse Core Ops, SparseCore 0:
  11.3 70.8 all-gather.10
  89.3 16.9 all-reduce.4
  114.5 146.9 reduce-scatter.2
  265.1 67.2 all-gather.6
  339.4 16.9 all-reduce.6
  359.6 69.3 all-gather.12
  441.3 16.9 all-reduce.8
  466.6 146.4 reduce-scatter.4
  616.8 67.2 all-gather.8
  691.2 16.9 all-reduce.10
where the time goes:
time: 730 us; the launch traced here: 729 us
  waiting for transfers between devices  613 us (84%)
  matrix products  96 us (13%)
  between operations  14.2 us (2%)
    reduce_scatter x2, waiting for transfers between devices, local(): lax.psum_scatter(lax.dot_general(first_rows, second_half, (((1,), (1,)),...  294 us
    all_gather x2, waiting for transfers between devices, local(): lax.all_gather(inputs[round_index], 'replica', axis=0, tiled=True)  139 us
    all_gather x2, waiting for transfers between devices, local(): error_half = lax.all_gather(error_own, 'replica', axis=0, tiled=True)  138 us
    dot_general x2, matrix products, local(): lax.dot_general(error_half, first_rows, (((0,), (0,)), ((), ())), preferr...  25.9 us
    psum x2, waiting for transfers between devices, local(): lax.psum(first_terms.astype(jnp.bfloat16), 'dom').astype(jnp.float32)  22.8 us
    dot_general x2, matrix products, local(): lax.dot_general(first_error, round_batch, (((0,), (0,)), ((), ())), prefe...  21 us
    dot_general x2, matrix products, local(): lax.dot_general(round_batch, first_half, (((1,), (1,)), ((), ())), prefer...  19.1 us
    psum x2, waiting for transfers between devices, local(): lax.psum(back_terms.astype(jnp.bfloat16), 'dom').astype(jnp.float32)  18.9 us
  transfers between devices with their start and end apart: 10, of which 10 were waited for; matrix products, arithmetic and copies ran while one was open for 4% of the time, Pallas kernels for 0%

commit v1 on v0

--- a/solution.py
+++ b/solution.py
@@ -53,7 +53,9 @@
         back_terms = (
             jnp.dot(error_half, second_half, preferred_element_type=jnp.float32) * unit_scale
         )
-        back_pre = lax.psum(back_terms.astype(jnp.bfloat16), "dom").astype(jnp.float32)
+        back_pre = jnp.sum(lax.all_gather(back_terms.astype(jnp.bfloat16), "dom"), axis=0).astype(
+            jnp.float32
+        )
         first_error = (back_pre * (1.0 - first_out * first_out)).astype(jnp.bfloat16)
         first_grad = lax.dot_general(
             first_error, round_batch, (((0,), (0,)), ((), ())), preferred_element_type=jnp.float32

time: 730 us -> 706 us (0.967)
  waiting for transfers between devices: 613 us -> 580 us
    psum x2 -> x0, waiting for transfers between devices: 18.9 us -> none  [local(): lax.psum(back_terms.astype(jnp.bfloat16), 'dom').astype(jnp.float32)]
    all_gather x2, waiting for transfers between devices: 139 us -> 126 us  [local(): lax.all_gather(inputs[round_index], 'replica', axis=0, tiled=True)]
  transfers between devices with their start and end apart: 10 -> 8, of which waited for: 10 -> 8; matrix products, arithmetic and copies ran while one was open for 4% -> 4% of each run, Pallas kernels for 0% -> 0%
where the time goes in v1:
time: 706 us; the launch traced here: 705 us
  waiting for transfers between devices  580 us (82%)
  matrix products  95.6 us (14%)
  between operations  14.2 us (2%)
  other arithmetic  7.88 us (1%)
    reduce_scatter x2, waiting for transfers between devices, local(): lax.psum_scatter(lax.dot_general(first_rows, second_half, (((1,), (1,)),...  294 us
    all_gather x2, waiting for transfers between devices, local(): error_half = lax.all_gather(error_own, 'replica', axis=0, tiled=True)  137 us
    all_gather x2, waiting for transfers between devices, local(): lax.all_gather(inputs[round_index], 'replica', axis=0, tiled=True)  126 us
    dot_general x2, matrix products, local(): lax.dot_general(error_half, first_rows, (((0,), (0,)), ((), ())), preferr...  26.9 us
    psum x2, waiting for transfers between devices, local(): lax.psum(first_terms.astype(jnp.bfloat16), 'dom').astype(jnp.float32)  22.8 us
    dot_general x2, matrix products, local(): lax.dot_general(first_error, round_batch, (((0,), (0,)), ((), ())), prefe...  21 us
    dot_general x2, matrix products, local(): lax.dot_general(round_batch, first_half, (((1,), (1,)), ((), ())), prefer...  19.1 us
    dot_general x2, matrix products, local(): lax.dot_general(first_rows, second_half, (((1,), (1,)), ((), ())), prefer...  16.2 us
  transfers between devices with their start and end apart: 8, of which 8 were waited for; matrix products, arithmetic and copies ran while one was open for 4% of the time, Pallas kernels for 0%

profile of v1, /device:TPU:0, one launch (start us, length us, event | category | flops | bytes accessed | tf_op | source)
XLA Modules:
  0.0 705.4 jit_solution(4661089530813263027)
XLA Ops:
  7.2 1.8 fusion.71
  9.1 73.1 %all-gather.13.cloned.1.call-done = bf16[1,384,4096]{2,1,0:T(8,128)(2,1)} async-done(((bf16[1,24,4096]{2,1,0:T(8,128)(2,1)}), bf16[1,384,4096]{2,1,0:T(8,128)(2,1)}) %all-gather.13.cloned.1.call-update) | async-done | bytes 3145744 | tf_op jit(solution)/shard_map/all_gather | solution.py:17
  82.2 6.9 fusion.37
  89.2 17.1 %all-reduce.3.cloned.1.call-done = bf16[384,512]{1,0:T(8,128)(2,1)} async-done(((bf16[384,512]{1,0:T(8,128)(2,1)}), bf16[384,512]{1,0:T(8,128)(2,1)}) %all-reduce.3.cloned.1.call-update) | async-done | bytes 393232 | tf_op jit(solution)/shard_map/psum | solution.py:28
  106.3 8.1 %convolution_multiply_fusion.1 = f32[384,4096]{1,0:T(8,128)} fusion(f32[4096,512]{1,0:T(8,128)} %param.10, bf16[384,512]{1,0:T(8,128)(2,1)} %all-reduce.3.cloned.1.call-done), kind=kOutput, calls=%fused_computation.9 | convolution fusion | flops 1614675968 | bytes 15073280 | tf_op jit(solution)/shard_map/dot_general | solution.py:32
  114.5 147.1 %reduce-scatter.3.cloned.1.call-done = f32[24,4096]{1,0:T(8,128)} async-done(((f32[384,4096]{1,0:T(8,128)}), f32[24,4096]{1,0:T(8,128)}) %reduce-scatter.3.cloned.1.call-update) | async-done | bytes 393232 | tf_op jit(solution)/shard_map/reduce_scatter | solution.py:31
  261.5 1.8 fusion.60
  264.0 68.4 %all-gather.9.cloned.1.call-done = bf16[384,4096]{1,0:T(8,128)(2,1)} async-done(((bf16[24,4096]{1,0:T(8,128)(2,1)}), bf16[384,4096]{1,0:T(8,128)(2,1)}) %all-gather.9.cloned.1.call-update) | async-done | bytes 3145744 | tf_op jit(solution)/shard_map/all_gather | solution.py:49
  332.4 6.1 fusion.45
  338.5 2.5 all-gather.1
  341.0 2.1 reduce_sum.24
  343.2 6.8 fusion.7
  350.0 52.7 %all-gather.15.cloned.1.call-done = bf16[1,384,4096]{2,1,0:T(8,128)(2,1)} async-done(((bf16[1,24,4096]{2,1,0:T(8,128)(2,1)}), bf16[1,384,4096]{2,1,0:T(8,128)(2,1)}) %all-gather.15.cloned.1.call-update) | async-done | bytes 3145744 | tf_op jit(solution)/shard_map/all_gather | solution.py:17
  402.6 12.2 %fusion.48 = bf16[384,512]{1,0:T(8,128)(2,1)} fusion(bf16[1,384,4096]{2,1,0:T(8,128)(2,1)} %all-gather.15.cloned.1.call-done, f32[512,4096]{1,0:T(8,128)} %param.8, f32[512,4096]{1,0:T(8,128)} %fusion.7, f32[512,4096]{1,0:T(8,128)} %param.9), kind=kOutput, calls=%fused_computation.34 | convolution fusion | flops 1623588864 | bytes 28704768 | tf_op jit(solution)/shard_map/dot_general | solution.py:20
  415.1 11.2 %multiply_subtract_fusion.2 = (f32[4096,512]{1,0:T(8,128)}, f32[4096,512]{1,0:T(8,128)}) fusion(f32[4096,512]{1,0:T(8,128)} %param.10, f32[4096,512]{1,0:T(8,128)} %param.11, bf16[384,4096]{1,0:T(8,128)(2,1)S(1)} %copy-done.1, bf16[384,512]{1,0:T(8,128)(2,1)S(1)} %copy-done.5), kind=kOutput, calls=%fused_computation.4 | convolution fusion | flops 1621491712 | bytes 37093376 | tf_op jit(solution)/shard_map/dot_general | solution.py:50
  426.3 5.7 all-reduce.5.cloned.1.call-done
  432.0 8.1 %convolution_multiply_fusion = f32[384,4096]{1,0:T(8,128)} fusion(f32[4096,512]{1,0:T(8,128)} %get-tuple-element.10, bf16[384,512]{1,0:T(8,128)(2,1)} %all-reduce.5.cloned.1.call-done), kind=kOutput, calls=%fused_computation.8 | convolution fusion | flops 1614675968 | bytes 15073280 | tf_op jit(solution)/shard_map/dot_general | solution.py:32
  440.2 146.9 %reduce-scatter.5.cloned.1.call-done = f32[24,4096]{1,0:T(8,128)} async-done(((f32[384,4096]{1,0:T(8,128)}), f32[24,4096]{1,0:T(8,128)}) %reduce-scatter.5.cloned.1.call-update) | async-done | bytes 393232 | tf_op jit(solution)/shard_map/reduce_scatter | solution.py:31
  588.9 68.8 %all-gather.11.cloned.1.call-done = bf16[384,4096]{1,0:T(8,128)(2,1)} async-done(((bf16[24,4096]{1,0:T(8,128)(2,1)}), bf16[384,4096]{1,0:T(8,128)(2,1)}) %all-gather.11.cloned.1.call-update) | async-done | bytes 3145744 | tf_op jit(solution)/shard_map/all_gather | solution.py:49
  657.7 6.3 fusion.42
  664.0 2.5 all-gather.3
  666.5 2.1 reduce_sum.25
  668.6 15.7 %multiply_subtract_fusion = (f32[4096,512]{1,0:T(8,128)}, f32[4096,512]{1,0:T(8,128)}) fusion(f32[4096,512]{1,0:T(8,128)} %get-tuple-element.10, f32[4096,512]{1,0:T(8,128)} %param.11, f32[4096,512]{1,0:T(8,128)} %get-tuple-element.11, bf16[384,4096]{1,0:T(8,128)(2,1)S(1)} %copy-done.3, bf16[384,512]{1,0:T(8,128)(2,1)S(1)} %copy-done.4), kind=kOutput, calls=%fused_computation | convolution fusion | flops 1625686016 | bytes 45481984 | tf_op jit(solution)/shard_map/dot_general | solution.py:50
  684.3 14.2 %multiply_subtract_fusion.1 = (f32[512,4096]{1,0:T(8,128)}, f32[512,4096]{1,0:T(8,128)}) fusion(f32[512,4096]{1,0:T(8,128)} %param.8, f32[512,4096]{1,0:T(8,128)} %param.9, f32[512,4096]{1,0:T(8,128)} %fusion.7, bf16[1,384,4096]{2,1,0:T(8,128)(2,1)S(1)} %copy-done, bf16[384,512]{1,0:T(8,128)(2,1)S(1)} %copy-done.6, bf16[384,512]{1,0:T(8,128)(2,1)S(1)} %copy-done.4), kind=kOutput, calls=%fused_computation.2 | convolution fusion | flops 1632763904 | bytes 45875200 | tf_op jit(solution)/shard_map/dot_general | solution.py:60
  (33 shorter events, 3.0 us)
Async XLA Ops:
  7.2 75.1 %all-gather.13.cloned.1.call-start = ((), (), s32[]{:S(2)}) async-start(), calls=%async_computation.8 | async-start | bytes 3342336 | tf_op jit(solution)/shard_map/all_gather | solution.py:17
  9.0 97.3 %all-reduce.3.cloned.1.call-start = ((), (), s32[]{:S(2)}) async-start(), calls=%async_computation.2 | async-start | bytes 786432 | tf_op jit(solution)/shard_map/psum | solution.py:28
  89.2 172.4 %reduce-scatter.3.cloned.1.call-start = ((), (), s32[]{:S(2)}) async-start(), calls=%async_computation.3 | async-start | bytes 6684672 | tf_op jit(solution)/shard_map/reduce_scatter | solution.py:31
  114.4 228.8 %copy-start.2 = (bf16[1,384,4096]{2,1,0:T(8,128)(2,1)S(1)}, bf16[1,384,4096]{2,1,0:T(8,128)(2,1)}, u32[]{:S(2)}) copy-start(bf16[1,384,4096]{2,1,0:T(8,128)(2,1)} %all-gather.13.cloned.1.call-done) | copy-start | bytes 9437188
  114.4 228.8 %copy-start.5 = (bf16[384,512]{1,0:T(8,128)(2,1)S(1)}, bf16[384,512]{1,0:T(8,128)(2,1)}, u32[]{:S(2)}) copy-start(bf16[384,512]{1,0:T(8,128)(2,1)} %all-reduce.3.cloned.1.call-done) | copy-start | bytes 1179652
  114.4 218.0 %all-gather.9.cloned.1.call-start = ((), (), s32[]{:S(2)}) async-start(), calls=%async_computation.4 | async-start | bytes 3342336 | tf_op jit(solution)/shard_map/all_gather | solution.py:49
  263.4 139.3 %all-gather.15.cloned.1.call-start = ((), (), s32[]{:S(2)}) async-start(), calls=%async_computation.9 | async-start | bytes 3342336 | tf_op jit(solution)/shard_map/all_gather | solution.py:17
  264.0 168.0 %all-reduce.5.cloned.1.call-start = ((), (), s32[]{:S(2)}) async-start(), calls=%async_computation.5 | async-start | bytes 786432 | tf_op jit(solution)/shard_map/psum | solution.py:28
  350.0 65.1 %copy-start.1 = (bf16[384,4096]{1,0:T(8,128)(2,1)S(1)}, bf16[384,4096]{1,0:T(8,128)(2,1)}, u32[]{:S(2)}) copy-start(bf16[384,4096]{1,0:T(8,128)(2,1)} %all-gather.9.cloned.1.call-done) | copy-start | bytes 9437188
  414.8 172.2 %reduce-scatter.5.cloned.1.call-start = ((), (), s32[]{:S(2)}) async-start(), calls=%async_computation.6 | async-start | bytes 6684672 | tf_op jit(solution)/shard_map/reduce_scatter | solution.py:31
  432.0 155.1 %copy-start.7 = (bf16[2,24,4096]{2,1,0:T(8,128)(2,1)S(1)}, bf16[2,24,4096]{2,1,0:T(8,128)(2,1)}, u32[]{:S(2)}) copy-start(bf16[2,24,4096]{2,1,0:T(8,128)(2,1)} %param.7) | copy-start | bytes 1179652
  440.1 228.5 %copy-start.4 = (bf16[384,512]{1,0:T(8,128)(2,1)S(1)}, bf16[384,512]{1,0:T(8,128)(2,1)}, u32[]{:S(2)}) copy-start(bf16[384,512]{1,0:T(8,128)(2,1)} %all-reduce.5.cloned.1.call-done) | copy-start | bytes 1179652
  440.1 217.6 %all-gather.11.cloned.1.call-start = ((), (), s32[]{:S(2)}) async-start(), calls=%async_computation.7 | async-start | bytes 3342336 | tf_op jit(solution)/shard_map/all_gather | solution.py:49
  657.7 10.9 %copy-start.3 = (bf16[384,4096]{1,0:T(8,128)(2,1)S(1)}, bf16[384,4096]{1,0:T(8,128)(2,1)}, u32[]{:S(2)}) copy-start(bf16[384,4096]{1,0:T(8,128)(2,1)} %all-gather.11.cloned.1.call-done) | copy-start | bytes 9437188
  668.6 15.7 %copy-start = (bf16[1,384,4096]{2,1,0:T(8,128)(2,1)S(1)}, bf16[1,384,4096]{2,1,0:T(8,128)(2,1)}, u32[]{:S(2)}) copy-start(bf16[1,384,4096]{2,1,0:T(8,128)(2,1)} %all-gather.15.cloned.1.call-done) | copy-start | bytes 9437188
  668.6 15.7 %copy-start.6 = (bf16[384,512]{1,0:T(8,128)(2,1)S(1)}, bf16[384,512]{1,0:T(8,128)(2,1)}, u32[]{:S(2)}) copy-start(bf16[384,512]{1,0:T(8,128)(2,1)} %reduce_sum.25) | copy-start | bytes 1179652
Sparse Core Ops, SparseCore 0:
  11.3 70.8 all-gather.12
  89.3 16.9 all-reduce.2
  114.5 146.9 reduce-scatter.2
  265.1 67.2 all-gather.8
  336.0 66.6 all-gather.14
  415.0 16.9 all-reduce.4
  440.2 146.7 reduce-scatter.4
  590.4 67.2 all-gather.10
